TPU v7x, 512 devices: a whole 4x8x8 slice. The times are simulated.
512 devices in a mesh: pipe: 8 (over y_lo, x), expert: 64 (over y_hi, z, core).
Axes of the slice: x: 4, y: 8 (y_hi: 4, y_lo: 2; y = y_hi * 2 + y_lo), z: 8, core: 2. Of those that a mesh axis runs over, the one named last changes fastest.
Arguments:
- state: bfloat16 [64, 8, 128, 2048], P('expert', 'pipe'), may hold values from -24 to 24
- query: bfloat16 [64, 8, 128, 2048], P('expert', 'pipe'), may hold values from -8 to 8
- enc_kv: bfloat16 [64, 256, 2, 2048], P('expert', 'pipe'), may hold values from -4 to 4
- gain: float32 [2048], replicated, may hold values from 0.1 to 1.9
- w_in: bfloat16 [2048, 24576], P(None, 'expert'), may hold values from -0.125 to 0.125
- w_out: bfloat16 [24576, 2048], P('expert'), may hold values from -0.109375 to 0.109375
- expert_id: int32 [64, 8, 128], P('expert', 'pipe'), may hold values from 0 to 7
- slot: int32 [64, 8, 128], P('expert', 'pipe'), may hold values from -1 to 23, as said below
- gate: float32 [64, 8, 128], P('expert', 'pipe'), may hold values from 0.3 to 1
Outputs:
- output: bfloat16 [64, 8, 128, 2048], P('expert', 'pipe')
Inputs may be any that keep to these rules, and one draw needn't show every extreme that they name: Within the 128 tokens of one source and sample, the tokens sent to one expert take slots 0, 1, 2, ... in token order until 24 are taken; later ones have slot -1. In every draw some expert is given 24 slotted tokens by every source and sample.
All inputs are finite; a program needn't handle non-finite values.
Results may differ from a plain program's by a relative error of at most 0.0055.
Values may be sent and summed in bfloat16 or wider, within the bound.
A program may use at most 128 MiB of HBM per device.

v0:
```python
import math
import jax
import jax.numpy as jnp
from jax import lax
from jax.sharding import PartitionSpec as P

HEADS = 16
HD = 128
WSPLIT = 8


def expert_ffn(slot_rows, w_in, w_out):
    senders, slots_here, width = slot_rows.shape
    flat_rows = slot_rows.reshape(senders * slots_here, width)
    activation = jnp.maximum(
        jnp.dot(flat_rows, w_in, preferred_element_type=jnp.float32), 0.0
    ).astype(jnp.bfloat16)
    partial_value = jnp.dot(activation, w_out, preferred_element_type=jnp.float32).astype(
        jnp.bfloat16
    )
    return partial_value.reshape(senders, slots_here, width)


def body(state, query, enc_kv, gain, w_in, w_out, expert_id, slot, gate):
    tokens = state.shape[2]
    width = state.shape[3]
    queries = query.reshape(tokens, HEADS, HD)
    scale = 1.0 / math.sqrt(HD)
    kv_piece = lax.all_gather(enc_kv, "pipe", axis=1, tiled=True)
    best_score = jnp.full((HEADS, tokens), -jnp.inf, jnp.float32)
    denominator = jnp.zeros((HEADS, tokens), jnp.float32)
    accumulated = jnp.zeros((HEADS, tokens, HD), jnp.float32)
    key_rows = kv_piece[0, :, 0].reshape(-1, HEADS, HD)
    value_rows = kv_piece[0, :, 1].reshape(-1, HEADS, HD)
    scores = (
        jnp.einsum("thd,lhd->htl", queries, key_rows, preferred_element_type=jnp.float32) * scale
    )
    new_best = jnp.max(scores, axis=2)
    factor = jnp.exp(best_score - new_best)
    raised = jnp.exp(scores - new_best[:, :, None])
    denominator = denominator * factor + jnp.sum(raised, axis=2)
    update = jnp.einsum(
        "htl,lhd->htd", raised.astype(jnp.bfloat16), value_rows, preferred_element_type=jnp.float32
    )
    best_score, denominator, accumulated = (
        new_best,
        denominator,
        accumulated * factor[:, :, None] + update,
    )
    attended = jnp.transpose(accumulated / denominator[:, :, None], (1, 0, 2)).reshape(
        tokens, width
    )
    hidden_state = state[0, 0].astype(jnp.float32) + attended
    mean_square = jnp.mean(hidden_state * hidden_state, axis=-1, keepdims=True)
    normed = (hidden_state * lax.rsqrt(mean_square + 1e-06) * gain).astype(jnp.bfloat16)
    experts = lax.axis_size("expert") // WSPLIT
    capacity = 3 * tokens // (2 * experts)
    flat_slot = jnp.where(slot[0, 0] >= 0, expert_id[0, 0] * capacity + slot[0, 0], -1)
    slot_ids = jnp.arange(experts * capacity, dtype=jnp.int32)
    selector = (slot_ids[:, None] == flat_slot[None, :]).astype(jnp.bfloat16)
    packed = jnp.dot(selector, normed, preferred_element_type=jnp.float32).astype(jnp.bfloat16)
    copies = jnp.broadcast_to(
        packed.reshape(experts, 1, capacity, width), (experts, WSPLIT, capacity, width)
    )
    copies = copies.reshape(experts * WSPLIT, capacity, width)
    partial_value = expert_ffn(
        lax.all_to_all(copies, "expert", split_axis=0, concat_axis=0, tiled=True), w_in, w_out
    )
    returned = lax.all_to_all(partial_value, "expert", split_axis=0, concat_axis=0, tiled=True)
    summed = jnp.sum(returned.reshape(experts, WSPLIT, capacity, width), axis=1, dtype=jnp.float32)
    summed = summed.reshape(experts * capacity, width)
    picked = jnp.take(summed, jnp.maximum(flat_slot, 0), axis=0)
    contribution = jnp.where((flat_slot >= 0)[:, None], gate[0, 0][:, None] * picked, 0.0)
    output = (hidden_state + contribution).astype(jnp.bfloat16)
    return output.reshape(1, 1, tokens, width)


def solution(mesh):
    return jax.shard_map(
        body,
        mesh=mesh,
        in_specs=(
            P("expert", "pipe", None, None),
            P("expert", "pipe", None, None),
            P("expert", "pipe", None, None),
            P(),
            P(None, "expert"),
            P("expert", None),
            P("expert", "pipe", None),
            P("expert", "pipe", None),
            P("expert", "pipe", None),
        ),
        out_specs=P("expert", "pipe", None, None),
        check_vma=False,
    )
```

profile of v0, /device:TPU:288, one launch (start us, length us, event | category | flops | bytes accessed | tf_op | source)
XLA Modules:
  0.0 509.5 jit_solution(5332171025868441447)
XLA Ops:
  6.5 0.0 copy-start
  6.5 0.0 all-gather.2.cloned.1.call-start
  6.5 0.7 all-gather.2.cloned.1.call-update
  7.3 1.1 copy.31
  8.4 2.2 copy.28
  10.7 0.0 copy-done.6
  10.7 0.0 copy-done.5
  10.7 46.0 %all-gather.2.cloned.1.call-done = bf16[1,256,2,2048]{3,2,0,1:T(2,128)(2,1)} async-done(((bf16[1,32,2,2048]{3,2,0,1:T(2,128)(2,1)}), bf16[1,256,2,2048]{3,2,0,1:T(2,128)(2,1)}) %all-gather.2.cloned.1.call-update) | async-done | bytes 2097168 | tf_op jit(solution)/shard_map/all_gather | solution.py:29
  56.6 6.8 %fusion.24 = (bf16[1,256,1,2048]{3,2,0,1:T(2,128)(2,1)}, bf16[1,256,1,2048]{3,2,0,1:T(2,128)(2,1)}) fusion(bf16[1,256,2,2048]{3,2,0,1:T(2,128)(2,1)} %all-gather.2.cloned.1.call-done), kind=kLoop, calls=%fused_computation.42 | loop fusion | bytes 4194304 | tf_op jit(solution)/shard_map/slice | solution.py:33
  63.4 4.5 copy.30
  68.0 0.5 multiply_reduce_fusion
  68.5 1.3 copy-done.1
  69.8 0.8 fusion.1
  70.6 5.8 %copy.25 = bf16[1,256,1,2048]{1,3,2,0:T(8,128)(2,1)} copy(bf16[1,256,1,2048]{3,2,0,1:T(2,128)(2,1)} %get-tuple-element.8) | data formatting | bytes 2097152 | tf_op jit(solution)/shard_map/slice | solution.py:34
  76.4 2.8 multiply_reduce_fusion.1
  79.2 0.0 copy-start.2
  79.2 0.0 copy-start.3
  79.2 1.3 copy.27
  80.5 0.0 copy-done.2
  80.5 0.0 copy-done.3
  80.5 1.7 convolution_convert_fusion.1
  82.2 0.8 broadcast_in_dim.54
  83.0 173.5 %all_to_all.10 = bf16[64,24,2048]{2,1,0:T(8,128)(2,1)} all-to-all(bf16[64,24,2048]{2,1,0:T(8,128)(2,1)S(1)} %bitcast.61), channel_id=1, replica_groups=mesh['pipe'=8,'expert'=64] {'expert'}, dimensions={0} | all-to-all | bytes 12582912 | tf_op jit(solution)/shard_map/all_to_all | solution.py:67
  256.5 10.9 %convolution_convert_fusion = bf16[1536,2048]{1,0:T(8,128)(2,1)} fusion(bf16[384,2048]{1,0:T(8,128)(2,1)S(1)} %copy-done, bf16[1536,2048]{1,0:T(8,128)(2,1)} %bitcast.63, bf16[2048,384]{1,0:T(8,128)(2,1)} %param.13), kind=kOutput, calls=%fused_computation.2 | convolution fusion | flops 4836163584 | bytes 15728640 | tf_op jit(solution)/shard_map/dot_general | solution.py:18
  267.4 12.9 %all-to-all-start.1 = ((bf16[64,24,2048]{2,1,0:T(8,128)(2,1)}), bf16[64,24,2048]{2,1,0:T(8,128)(2,1)}, u32[]{:S(2)}, u32[]{:S(2)}) async-start(bf16[64,24,2048]{2,1,0:T(8,128)(2,1)} %bitcast.62), calls=%async_computation.1 | async-start | bytes 12582912 | tf_op jit(solution)/shard_map/all_to_all | solution.py:69
  280.3 1.4 copy.26
  281.7 212.0 %all-to-all-done.1 = bf16[64,24,2048]{2,1,0:T(8,128)(2,1)} async-done(((bf16[64,24,2048]{2,1,0:T(8,128)(2,1)}), bf16[64,24,2048]{2,1,0:T(8,128)(2,1)}, u32[]{:S(2)}, u32[]{:S(2)}) %all-to-all-start.1) | async-done | bytes 6291488 | tf_op jit(solution)/shard_map/all_to_all | solution.py:69
  493.7 4.1 convert_reduce_fusion
  497.9 0.0 copy-start.4
  497.9 1.9 gather_fusion
  499.8 0.0 copy-done.4
  499.8 2.9 fusion.9
  (11 shorter events, 0.1 us)
Async XLA Ops:
  6.5 250.0 %copy-start = (bf16[384,2048]{1,0:T(8,128)(2,1)S(1)}, bf16[384,2048]{1,0:T(8,128)(2,1)}, u32[]{:S(2)}) copy-start(bf16[384,2048]{1,0:T(8,128)(2,1)} %param.14) | copy-start | bytes 4718596
  6.5 4.1 copy-start.6
  6.5 4.1 copy-start.5
  6.5 50.1 %all-gather.2.cloned.1.call-start = ((), (), s32[]{:S(2)}) async-start(), calls=%async_computation.2 | async-start | bytes 2359296 | tf_op jit(solution)/shard_map/all_gather | solution.py:29
  68.5 1.3 copy-start.1
  79.2 1.3 copy-start.2
  79.2 1.3 copy-start.3
  267.4 226.3 %all-to-all-start.1 = ((bf16[64,24,2048]{2,1,0:T(8,128)(2,1)}), bf16[64,24,2048]{2,1,0:T(8,128)(2,1)}, u32[]{:S(2)}, u32[]{:S(2)}) async-start(bf16[64,24,2048]{2,1,0:T(8,128)(2,1)} %bitcast.62), calls=%async_computation.1 | async-start | bytes 12582912 | tf_op jit(solution)/shard_map/all_to_all | solution.py:69
  497.9 1.9 copy-start.4
Sparse Core Ops, SparseCore 0:
  9.4 47.1 all-gather.1
where the time goes:
time: 510 us
  waiting for transfers between devices  259 us (51%)
  blocking collectives  174 us (34%)
  local copies, waits for them, and re-layouts  27.2 us (5%)
  matrix products  15.9 us (3%)
  between operations  13.5 us (3%)
  starting transfers between devices  12.9 us (3%)
  other arithmetic  7.85 us (2%)
    all_to_all x1, waiting for transfers between devices, body(): lax.all_to_all(partial_value, 'expert', split_axis=0, concat_axis=0, tile...  212 us
    all_to_all x1, blocking collectives, body(): lax.all_to_all(copies, 'expert', split_axis=0, concat_axis=0, tiled=True)  174 us
    all_gather x1, waiting for transfers between devices, body(): kv_piece = lax.all_gather(enc_kv, 'pipe', axis=1, tiled=True)  46 us
    all_to_all x1, starting transfers between devices, body(): lax.all_to_all(partial_value, 'expert', split_axis=0, concat_axis=0, tile...  12.9 us
    dot_general x1, matrix products, expert_ffn(): jnp.dot(activation, w_out, preferred_element_type=jnp.float32)  10.9 us
  transfers between devices with their start and end apart: 2, of which 2 were waited for; matrix products, arithmetic and copies ran while one was open for 1% of the time, Pallas kernels for 0%

commit v1 on v0

--- a/solution.py
+++ b/solution.py
@@ -26,7 +26,15 @@
     width = state.shape[3]
     queries = query.reshape(tokens, HEADS, HD)
     scale = 1.0 / math.sqrt(HD)
-    kv_piece = lax.all_gather(enc_kv, "pipe", axis=1, tiled=True)
+    kv_piece = jnp.concatenate(
+        lax.all_to_all(
+            jnp.stack([enc_kv for _ in range(lax.axis_size("pipe"))]),
+            concat_axis=0,
+            axis_name="pipe",
+            split_axis=0,
+        ),
+        axis=1,
+    )
     best_score = jnp.full((HEADS, tokens), -jnp.inf, jnp.float32)
     denominator = jnp.zeros((HEADS, tokens), jnp.float32)
     accumulated = jnp.zeros((HEADS, tokens, HD), jnp.float32)

time: 510 us -> 474 us (0.929)
  the two profiles are of different devices: /device:TPU:288 before, /device:TPU:36 now
where the time goes in v1:
time: 474 us; the launch traced here: 473 us
  waiting for transfers between devices  216 us (46%)
  blocking collectives  192 us (41%)
  starting transfers between devices  23.2 us (5%)
  local copies, waits for them, and re-layouts  17.5 us (4%)
  matrix products  16.9 us (4%)
  other arithmetic  7.85 us (2%)
    all_to_all x1, waiting for transfers between devices, body(): lax.all_to_all(partial_value, 'expert', split_axis=0, concat_axis=0, tile...  193 us
    all_to_all x1, blocking collectives, body(): lax.all_to_all(copies, 'expert', split_axis=0, concat_axis=0, tiled=True)  192 us
    all_to_all x1, waiting for transfers between devices, body(): lax.all_to_all(jnp.stack([enc_kv for _ in range(lax.axis_size('pipe'))]),...  22.5 us
    all_to_all x1, starting transfers between devices, body(): lax.all_to_all(partial_value, 'expert', split_axis=0, concat_axis=0, tile...  18.2 us
    dot_general x1, matrix products, expert_ffn(): jnp.dot(activation, w_out, preferred_element_type=jnp.float32)  10.9 us
  transfers between devices with their start and end apart: 2, of which 2 were waited for; matrix products, arithmetic and copies ran while one was open for 1% of the time, Pallas kernels for 0%

profile of v1, /device:TPU:36, one launch (start us, length us, event | category | flops | bytes accessed | tf_op | source)
XLA Modules:
  0.0 473.2 jit_solution(10939798223697935386)
XLA Ops:
  0.0 0.0 copy-start
  0.0 1.2 copy.23
  1.2 1.6 stack.2
  2.7 5.0 %all-to-all-start = ((bf16[8,1,32,2,2048]{4,2,3,1,0:T(8,128)(2,1)}), bf16[8,1,32,2,2048]{4,2,3,1,0:T(8,128)(2,1)}, u32[]{:S(2)}, u32[]{:S(2)}) async-start(bf16[8,1,32,2,2048]{4,2,3,1,0:T(8,128)(2,1)} %stack.2), calls=%async_computation | async-start | bytes 4194304 | tf_op jit(solution)/shard_map/all_to_all | solution.py:30
  7.8 0.0 copy-done.4
  7.8 0.9 copy.33
  8.7 0.0 copy-done.2
  8.7 1.2 copy.31
  9.9 0.0 copy-done.7
  9.9 0.0 copy-done.8
  9.9 22.5 %all-to-all-done = bf16[8,1,32,2,2048]{4,2,3,1,0:T(8,128)(2,1)} async-done(((bf16[8,1,32,2,2048]{4,2,3,1,0:T(8,128)(2,1)}), bf16[8,1,32,2,2048]{4,2,3,1,0:T(8,128)(2,1)}, u32[]{:S(2)}, u32[]{:S(2)}) %all-to-all-start) | async-done | bytes 2097184 | tf_op jit(solution)/shard_map/all_to_all | solution.py:30
  32.3 1.7 copy.24
  34.1 1.4 fusion.24
  35.5 1.5 copy.25
  37.0 1.5 multiply_reduce_fusion
  38.6 1.3 copy-done.1
  39.9 0.8 fusion.1
  40.7 0.0 copy-done.3
  40.7 1.3 copy.28
  42.0 2.8 multiply_reduce_fusion.1
  44.8 1.3 copy.30
  46.1 1.7 convolution_convert_fusion.1
  47.8 0.8 broadcast_in_dim.54
  48.6 191.8 %all_to_all.15 = bf16[64,24,2048]{2,1,0:T(8,128)(2,1)} all-to-all(bf16[64,24,2048]{2,1,0:T(8,128)(2,1)S(1)} %bitcast.62), channel_id=1, replica_groups=mesh['pipe'=8,'expert'=64] {'expert'}, dimensions={0} | all-to-all | bytes 12582912 | tf_op jit(solution)/shard_map/all_to_all | solution.py:75
  240.4 10.9 %convolution_convert_fusion = bf16[1536,2048]{1,0:T(8,128)(2,1)} fusion(bf16[384,2048]{1,0:T(8,128)(2,1)S(1)} %copy-done, bf16[1536,2048]{1,0:T(8,128)(2,1)} %bitcast.65, bf16[2048,384]{1,0:T(8,128)(2,1)} %param.13), kind=kOutput, calls=%fused_computation.2 | convolution fusion | flops 4836163584 | bytes 15728640 | tf_op jit(solution)/shard_map/dot_general | solution.py:18
  251.3 18.2 %all-to-all-start.2 = ((bf16[64,24,2048]{2,1,0:T(8,128)(2,1)}), bf16[64,24,2048]{2,1,0:T(8,128)(2,1)}, u32[]{:S(2)}, u32[]{:S(2)}) async-start(bf16[64,24,2048]{2,1,0:T(8,128)(2,1)} %bitcast.64), calls=%async_computation.2 | async-start | bytes 12582912 | tf_op jit(solution)/shard_map/all_to_all | solution.py:77
  269.5 1.4 copy.29
  270.9 193.3 %all-to-all-done.2 = bf16[64,24,2048]{2,1,0:T(8,128)(2,1)} async-done(((bf16[64,24,2048]{2,1,0:T(8,128)(2,1)}), bf16[64,24,2048]{2,1,0:T(8,128)(2,1)}, u32[]{:S(2)}, u32[]{:S(2)}) %all-to-all-start.2) | async-done | bytes 6291488 | tf_op jit(solution)/shard_map/all_to_all | solution.py:77
  464.2 4.1 convert_reduce_fusion
  468.3 0.0 copy-start.6
  468.3 1.9 gather_fusion
  470.3 2.9 fusion.9
  (17 shorter events, 0.1 us)
Async XLA Ops:
  0.0 240.4 %copy-start = (bf16[384,2048]{1,0:T(8,128)(2,1)S(1)}, bf16[384,2048]{1,0:T(8,128)(2,1)}, u32[]{:S(2)}) copy-start(bf16[384,2048]{1,0:T(8,128)(2,1)} %param.14) | copy-start | bytes 4718596
  2.7 5.1 %copy-start.4 = (bf16[1,1,128,2048]{3,2,1,0:T(8,128)(2,1)S(1)}, bf16[1,1,128,2048]{3,2,1,0:T(8,128)(2,1)}, u32[]{:S(2)}) copy-start(bf16[1,1,128,2048]{3,2,1,0:T(8,128)(2,1)} %param.10) | copy-start | bytes 1572868
  2.7 6.0 %copy-start.2 = (bf16[1,1,128,2048]{3,2,1,0:T(8,128)(2,1)S(1)}, bf16[1,1,128,2048]{3,2,1,0:T(8,128)(2,1)}, u32[]{:S(2)}) copy-start(bf16[1,1,128,2048]{3,2,1,0:T(8,128)(2,1)} %param.9) | copy-start | bytes 1572868
  2.7 29.6 %all-to-all-start = ((bf16[8,1,32,2,2048]{4,2,3,1,0:T(8,128)(2,1)}), bf16[8,1,32,2,2048]{4,2,3,1,0:T(8,128)(2,1)}, u32[]{:S(2)}, u32[]{:S(2)}) async-start(bf16[8,1,32,2,2048]{4,2,3,1,0:T(8,128)(2,1)} %stack.2), calls=%async_computation | async-start | bytes 4194304 | tf_op jit(solution)/shard_map/all_to_all | solution.py:30
  7.8 2.1 copy-start.7
  7.8 2.1 copy-start.8
  38.5 1.3 copy-start.1
  38.6 2.1 copy-start.3
  44.8 1.3 copy-start.5
  251.3 212.9 %all-to-all-start.2 = ((bf16[64,24,2048]{2,1,0:T(8,128)(2,1)}), bf16[64,24,2048]{2,1,0:T(8,128)(2,1)}, u32[]{:S(2)}, u32[]{:S(2)}) async-start(bf16[64,24,2048]{2,1,0:T(8,128)(2,1)} %bitcast.64), calls=%async_computation.2 | async-start | bytes 12582912 | tf_op jit(solution)/shard_map/all_to_all | solution.py:77
  468.3 1.9 copy-start.6
